TPU v7x, 128 devices: a whole 4x4x4 slice. The times are simulated.
128 devices in a mesh: gx: 16 (over z, y), gy: 8 (over x, core).
Axes of the slice: x: 4, y: 4, z: 4, core: 2. Of those that a mesh axis runs over, the one named last changes fastest.
Arguments:
- pumping: float32 [16, 4, 128, 1024], P(None, None, 'gx', 'gy'), may hold values from -1080 to 1080
- conductivity: float32 [4, 128, 1024], P(None, 'gx', 'gy'), may hold values from 0.2 to 5
- capacity: float32 [4, 128, 1024], P(None, 'gx', 'gy'), may hold values from 1 to 10
Outputs:
- solution: float32 [16, 4, 128, 1024], P(None, None, 'gx', 'gy')
- residual: float32 [16, 4, 128, 1024], P(None, None, 'gx', 'gy')
All inputs are finite; a program needn't handle non-finite values.
Results may differ from a plain program's by a relative error of at most 0.0035.
Values sent between devices are 32-bit elements; how exact they have to be, the bound alone decides.
A program may use at most 64 MiB of HBM per device.

v0:
```python
import jax
import jax.numpy as jnp
from jax import lax
from jax.sharding import PartitionSpec as P

RHS = 16
S = 4
CYCLES = 5
BASIS = 80


def padded_2(array, sides, width):
    for axis, dim in sides:
        devices, length = (lax.axis_size(axis), array.shape[dim])
        up = [(i, (i + 1) % devices) for i in range(devices - 1)]
        down = [(j, i) for i, j in up]
        last = lax.slice_in_dim(array, length - width, length, axis=dim)
        leading = lax.slice_in_dim(array, 0, width, axis=dim)
        before = lax.ppermute(last, axis, up)
        after = lax.ppermute(leading, axis, down)
        array = jnp.concatenate([before, array, after], axis=dim)
    return array


def halo_4(array):
    out = {}
    for axis, dim in (("gx", 2), ("gy", 3)):
        devices, length = (lax.axis_size(axis), array.shape[dim])
        up = [(i, (i + 1) % devices) for i in range(devices - 1)]
        down = [(j, i) for i, j in up]
        last = lax.slice_in_dim(array, length - 1, length, axis=dim)
        leading = lax.slice_in_dim(array, 0, 1, axis=dim)
        out[axis] = (lax.ppermute(last, axis, up), lax.ppermute(leading, axis, down))
    xb, xa = out["gx"]
    yb, ya = out["gy"]
    rows = jnp.concatenate([xb, array, xa], axis=2)
    zero_pad = ((0, 0), (0, 0), (1, 1), (0, 0))
    return jnp.concatenate([jnp.pad(yb, zero_pad), rows, jnp.pad(ya, zero_pad)], axis=3)


def face_terms(padded, storage):
    core = padded[1:-1, 1:-1, 1:-1]
    terms = (
        (core + padded[:-2, 1:-1, 1:-1]) * 0.5,
        (core + padded[2:, 1:-1, 1:-1]) * 0.5,
        (core + padded[1:-1, :-2, 1:-1]) * 0.5,
        (core + padded[1:-1, 2:, 1:-1]) * 0.5,
        (core + padded[1:-1, 1:-1, :-2]) * 0.5,
        (core + padded[1:-1, 1:-1, 2:]) * 0.5,
    )
    diagonal = storage + terms[0] + terms[1] + terms[2] + terms[3] + terms[4] + terms[5]
    return (terms, diagonal)


def apply_off(padded, terms):
    total = terms[0] * padded[:, :-2, 1:-1, 1:-1] + terms[1] * padded[:, 2:, 1:-1, 1:-1]
    total = total + terms[2] * padded[:, 1:-1, :-2, 1:-1] + terms[3] * padded[:, 1:-1, 2:, 1:-1]
    total = total + terms[4] * padded[:, 1:-1, 1:-1, :-2] + terms[5] * padded[:, 1:-1, 1:-1, 2:]
    return total


def small_solve(gram_all):
    shift_matrix = jnp.eye(BASIS, BASIS - RHS, dtype=jnp.float32) + jnp.eye(
        BASIS, BASIS - RHS, k=-RHS, dtype=jnp.float32
    )
    first_block = jnp.eye(BASIS, RHS, dtype=jnp.float32)
    hp = lax.Precision.HIGHEST
    gram_shift = jnp.dot(gram_all, shift_matrix, precision=hp)
    normal = jnp.dot(shift_matrix.T, gram_shift, precision=hp)
    right_side = jnp.dot(gram_shift.T, first_block, precision=hp)
    lower = jnp.linalg.cholesky(normal)
    y = jax.scipy.linalg.cho_solve((lower, True), right_side)
    coeffs = first_block - jnp.dot(shift_matrix, y, precision=hp)
    return (y, coeffs)


def shards(pumping, conductivity, capacity):
    hp = lax.Precision.HIGHEST
    shape = pumping.shape
    cond_halo = padded_2(conductivity, (("gx", 1), ("gy", 2)), 1)
    cond_pad = jnp.pad(cond_halo, ((1, 1), (0, 0), (0, 0)))
    terms, diagonal = face_terms(cond_pad, capacity)
    solution = jnp.zeros(shape, jnp.float32)
    residual = pumping / diagonal
    for restart in range(CYCLES):
        blocks = [residual]
        for k in range(S):
            bordered = halo_4(blocks[-1])
            padded = jnp.pad(bordered, ((0, 0), (1, 1), (0, 0), (0, 0)))
            blocks.append(-apply_off(padded, terms) / diagonal)
        stacked = jnp.concatenate(blocks, 0).reshape(BASIS, -1)
        local_gram = jnp.dot(stacked, stacked.T, precision=hp)
        gram_all = lax.psum(local_gram, ("gx", "gy"))
        y, coeffs = small_solve(gram_all)
        solution = solution + jnp.dot(y.T, stacked[: BASIS - RHS], precision=hp).reshape(shape)
        residual = jnp.dot(coeffs.T, stacked, precision=hp).reshape(shape)
    return (solution, residual)


def solution(mesh):
    return jax.shard_map(
        shards,
        mesh=mesh,
        in_specs=(P(None, None, "gx", "gy"), P(None, "gx", "gy"), P(None, "gx", "gy")),
        out_specs=(P(None, None, "gx", "gy"), P(None, None, "gx", "gy")),
        check_vma=False,
    )
```

profile of v0, /device:TPU:1, one launch (start us, length us, event | category | flops | bytes accessed | tf_op | source)
XLA Modules:
  0.0 819.0 jit_solution(14355877820562168291)
XLA Ops:
  1.4 4.0 collective-permute-start
  6.8 3.0 collective-permute-done.1
  10.6 5.1 collective-permute-start.2
  17.6 3.3 collective-permute-done.3
  23.9 3.2 collective-permute-start.5
  34.1 4.4 collective-permute-done.7
  39.3 4.3 collective-permute-start.9
  50.4 4.4 collective-permute-done.11
  55.6 5.2 collective-permute-start.13
  67.6 4.4 collective-permute-done.15
  72.9 4.3 collective-permute-start.17
  83.9 4.4 collective-permute-done.19
  90.7 75.5 %psum.35 = f32[80,80]{1,0:T(8,128)S(1)} all-reduce(f32[80,80]{1,0:T(8,128)S(1)} %convolution_bitcast_fusion.4), channel_id=1, replica_groups=mesh['gx'=16,'gy'=8] {'gx','gy'}, use_global_device_ids=true, to_apply=%region_0.1 | all-reduce | flops 6400 | bytes 51200 | tf_op jit(solution)/shard_map/psum | solution.py:93
  168.1 5.8 cholesky.89
  175.3 4.9 custom-call.11
  185.5 3.8 collective-permute-start.20
  192.7 4.4 collective-permute-done.23
  197.9 4.3 collective-permute-start.25
  209.0 4.4 collective-permute-done.27
  214.2 4.3 collective-permute-start.29
  225.2 4.4 collective-permute-done.31
  230.5 4.3 collective-permute-start.33
  238.2 2.5 collective-permute-start.35
  241.5 4.4 collective-permute-done.35
  249.4 73.8 %psum.36 = f32[80,80]{1,0:T(8,128)S(1)} all-reduce(f32[80,80]{1,0:T(8,128)S(1)} %convolution_bitcast_fusion.3), channel_id=1, replica_groups=mesh['gx'=16,'gy'=8] {'gx','gy'}, use_global_device_ids=true, to_apply=%region_3.6 | all-reduce | flops 6400 | bytes 51200 | tf_op jit(solution)/shard_map/psum | solution.py:93
  327.5 5.8 cholesky.100
  334.7 4.9 custom-call.12
  340.3 2.7 constant_dynamic-update-slice_fusion.11
  345.8 3.8 collective-permute-start.36
  352.9 4.4 collective-permute-done.39
  358.2 4.3 collective-permute-start.41
  369.2 4.4 collective-permute-done.43
  374.4 4.3 collective-permute-start.45
  385.5 4.4 collective-permute-done.47
  390.9 4.5 collective-permute-start.49
  403.6 2.8 collective-permute-done.51
  409.9 73.9 %psum.37 = f32[80,80]{1,0:T(8,128)S(1)} all-reduce(f32[80,80]{1,0:T(8,128)S(1)} %convolution_bitcast_fusion.2), channel_id=1, replica_groups=mesh['gx'=16,'gy'=8] {'gx','gy'}, use_global_device_ids=true, to_apply=%region_4.7 | all-reduce | flops 6400 | bytes 51200 | tf_op jit(solution)/shard_map/psum | solution.py:93
  488.1 5.8 cholesky.111
  495.3 4.9 custom-call.13
  500.9 2.8 constant_dynamic-update-slice_fusion.15
  506.5 4.3 collective-permute-start.52
  510.8 2.3 collective-permute-start.55
  514.4 4.1 collective-permute-done.55
  519.5 4.3 collective-permute-start.57
  531.0 3.8 collective-permute-done.59
  535.8 4.3 collective-permute-start.61
  546.9 4.2 collective-permute-done.63
  552.1 4.3 collective-permute-start.65
  564.5 2.8 collective-permute-done.67
  569.8 73.8 %psum.38 = f32[80,80]{1,0:T(8,128)S(1)} all-reduce(f32[80,80]{1,0:T(8,128)S(1)} %convolution_bitcast_fusion.1), channel_id=1, replica_groups=mesh['gx'=16,'gy'=8] {'gx','gy'}, use_global_device_ids=true, to_apply=%region_5.8 | all-reduce | flops 6400 | bytes 51200 | tf_op jit(solution)/shard_map/psum | solution.py:93
  645.5 5.8 cholesky.122
  652.7 4.9 custom-call.14
  662.6 4.1 collective-permute-start.68
  670.0 4.4 collective-permute-done.71
  675.4 4.3 collective-permute-start.73
  686.9 3.8 collective-permute-done.75
  691.6 4.3 collective-permute-start.77
  699.3 2.5 collective-permute-start.79
  703.0 3.9 collective-permute-done.79
  707.9 4.3 collective-permute-start.81
  719.5 3.8 collective-permute-done.83
  725.7 74.1 %psum.39 = f32[80,80]{1,0:T(8,128)S(1)} all-reduce(f32[80,80]{1,0:T(8,128)S(1)} %convolution_bitcast_fusion), channel_id=1, replica_groups=mesh['gx'=16,'gy'=8] {'gx','gy'}, use_global_device_ids=true, to_apply=%region_6.9 | all-reduce | flops 6400 | bytes 51200 | tf_op jit(solution)/shard_map/psum | solution.py:93
  801.7 5.8 cholesky.133
  808.9 4.9 custom-call.15
  (357 shorter events, 196.5 us)
Async XLA Ops:
  23.9 14.6 %collective-permute-start.5 = (f32[16,4,1,128]{3,0,2,1:T(8,128)S(1)}, f32[16,4,1,128]{3,0,2,1:T(8,128)S(1)}, u32[]{:S(2)}, u32[]{:S(2)}) collective-permute-start(f32[16,4,1,128]{3,0,2,1:T(8,128)S(1)} %get-tuple-element.125), channel_id=1, source_target_pairs={{0,8},{8,16},{16,24},{24,32},{32,40},{40,48},{48,56},{56,64},{64,7... | collective-permute-start | bytes 98312 | tf_op jit(solution)/shard_map/ppermute | solution.py:33
  27.1 11.4 %collective-permute-start.6 = (f32[16,4,1,128]{3,0,2,1:T(8,128)S(1)}, f32[16,4,1,128]{3,0,2,1:T(8,128)S(1)}, u32[]{:S(2)}, u32[]{:S(2)}) collective-permute-start(f32[16,4,1,128]{3,0,2,1:T(8,128)S(1)} %get-tuple-element.126), channel_id=1, source_target_pairs={{8,0},{16,8},{24,16},{32,24},{40,32},{48,40},{56,48},{64,56},{72,6... | collective-permute-start | bytes 98312 | tf_op jit(solution)/shard_map/ppermute | solution.py:33
  30.8 7.7 collective-permute-start.7
  39.3 15.5 %collective-permute-start.9 = (f32[16,4,1,128]{3,0,2,1:T(8,128)S(1)}, f32[16,4,1,128]{3,0,2,1:T(8,128)S(1)}, u32[]{:S(2)}, u32[]{:S(2)}) collective-permute-start(f32[16,4,1,128]{3,0,2,1:T(8,128)S(1)} %get-tuple-element.121), channel_id=1, source_target_pairs={{0,8},{8,16},{16,24},{24,32},{32,40},{40,48},{48,56},{56,64},{64,7... | collective-permute-start | bytes 98312 | tf_op jit(solution)/shard_map/ppermute | solution.py:33
  43.6 11.2 %collective-permute-start.10 = (f32[16,4,1,128]{3,0,2,1:T(8,128)S(1)}, f32[16,4,1,128]{3,0,2,1:T(8,128)S(1)}, u32[]{:S(2)}, u32[]{:S(2)}) collective-permute-start(f32[16,4,1,128]{3,0,2,1:T(8,128)S(1)} %get-tuple-element.122), channel_id=1, source_target_pairs={{8,0},{16,8},{24,16},{32,24},{40,32},{48,40},{56,48},{64,56},{72,6... | collective-permute-start | bytes 98312 | tf_op jit(solution)/shard_map/ppermute | solution.py:33
  47.0 7.7 collective-permute-start.11
  55.6 16.4 %collective-permute-start.13 = (f32[16,4,1,128]{3,0,2,1:T(8,128)S(1)}, f32[16,4,1,128]{3,0,2,1:T(8,128)S(1)}, u32[]{:S(2)}, u32[]{:S(2)}) collective-permute-start(f32[16,4,1,128]{3,0,2,1:T(8,128)S(1)} %get-tuple-element.117), channel_id=1, source_target_pairs={{0,8},{8,16},{16,24},{24,32},{32,40},{40,48},{48,56},{56,64},{64,7... | collective-permute-start | bytes 98312 | tf_op jit(solution)/shard_map/ppermute | solution.py:33
  60.8 11.2 %collective-permute-start.14 = (f32[16,4,1,128]{3,0,2,1:T(8,128)S(1)}, f32[16,4,1,128]{3,0,2,1:T(8,128)S(1)}, u32[]{:S(2)}, u32[]{:S(2)}) collective-permute-start(f32[16,4,1,128]{3,0,2,1:T(8,128)S(1)} %get-tuple-element.118), channel_id=1, source_target_pairs={{8,0},{16,8},{24,16},{32,24},{40,32},{48,40},{56,48},{64,56},{72,6... | collective-permute-start | bytes 98312 | tf_op jit(solution)/shard_map/ppermute | solution.py:33
  64.3 7.7 collective-permute-start.15
  72.9 15.3 %collective-permute-start.17 = (f32[16,4,1,128]{3,0,2,1:T(8,128)S(1)}, f32[16,4,1,128]{3,0,2,1:T(8,128)S(1)}, u32[]{:S(2)}, u32[]{:S(2)}) collective-permute-start(f32[16,4,1,128]{3,0,2,1:T(8,128)S(1)} %get-tuple-element.113), channel_id=1, source_target_pairs={{0,8},{8,16},{16,24},{24,32},{32,40},{40,48},{48,56},{56,64},{64,7... | collective-permute-start | bytes 98312 | tf_op jit(solution)/shard_map/ppermute | solution.py:33
  77.2 11.1 %collective-permute-start.18 = (f32[16,4,1,128]{3,0,2,1:T(8,128)S(1)}, f32[16,4,1,128]{3,0,2,1:T(8,128)S(1)}, u32[]{:S(2)}, u32[]{:S(2)}) collective-permute-start(f32[16,4,1,128]{3,0,2,1:T(8,128)S(1)} %get-tuple-element.114), channel_id=1, source_target_pairs={{8,0},{16,8},{24,16},{32,24},{40,32},{48,40},{56,48},{64,56},{72,6... | collective-permute-start | bytes 98312 | tf_op jit(solution)/shard_map/ppermute | solution.py:33
  80.6 7.7 collective-permute-start.19
  182.4 14.7 %collective-permute-start.21 = (f32[16,4,1,128]{3,0,2,1:T(8,128)S(1)}, f32[16,4,1,128]{3,0,2,1:T(8,128)S(1)}, u32[]{:S(2)}, u32[]{:S(2)}) collective-permute-start(f32[16,4,1,128]{3,0,2,1:T(8,128)S(1)} %get-tuple-element.109), channel_id=1, source_target_pairs={{0,8},{8,16},{16,24},{24,32},{32,40},{40,48},{48,56},{56,64},{64,7... | collective-permute-start | bytes 98312 | tf_op jit(solution)/shard_map/ppermute | solution.py:33
  184.1 13.0 %collective-permute-start.22 = (f32[16,4,1,128]{3,0,2,1:T(8,128)S(1)}, f32[16,4,1,128]{3,0,2,1:T(8,128)S(1)}, u32[]{:S(2)}, u32[]{:S(2)}) collective-permute-start(f32[16,4,1,128]{3,0,2,1:T(8,128)S(1)} %get-tuple-element.110), channel_id=1, source_target_pairs={{8,0},{16,8},{24,16},{32,24},{40,32},{48,40},{56,48},{64,56},{72,6... | collective-permute-start | bytes 98312 | tf_op jit(solution)/shard_map/ppermute | solution.py:33
  185.5 7.1 collective-permute-start.20
  189.4 7.7 collective-permute-start.23
  197.9 15.5 %collective-permute-start.25 = (f32[16,4,1,128]{3,0,2,1:T(8,128)S(1)}, f32[16,4,1,128]{3,0,2,1:T(8,128)S(1)}, u32[]{:S(2)}, u32[]{:S(2)}) collective-permute-start(f32[16,4,1,128]{3,0,2,1:T(8,128)S(1)} %get-tuple-element.105), channel_id=1, source_target_pairs={{0,8},{8,16},{16,24},{24,32},{32,40},{40,48},{48,56},{56,64},{64,7... | collective-permute-start | bytes 98312 | tf_op jit(solution)/shard_map/ppermute | solution.py:33
  202.2 11.2 %collective-permute-start.26 = (f32[16,4,1,128]{3,0,2,1:T(8,128)S(1)}, f32[16,4,1,128]{3,0,2,1:T(8,128)S(1)}, u32[]{:S(2)}, u32[]{:S(2)}) collective-permute-start(f32[16,4,1,128]{3,0,2,1:T(8,128)S(1)} %get-tuple-element.106), channel_id=1, source_target_pairs={{8,0},{16,8},{24,16},{32,24},{40,32},{48,40},{56,48},{64,56},{72,6... | collective-permute-start | bytes 98312 | tf_op jit(solution)/shard_map/ppermute | solution.py:33
  205.6 7.7 collective-permute-start.27
  214.2 15.5 %collective-permute-start.29 = (f32[16,4,1,128]{3,0,2,1:T(8,128)S(1)}, f32[16,4,1,128]{3,0,2,1:T(8,128)S(1)}, u32[]{:S(2)}, u32[]{:S(2)}) collective-permute-start(f32[16,4,1,128]{3,0,2,1:T(8,128)S(1)} %get-tuple-element.101), channel_id=1, source_target_pairs={{0,8},{8,16},{16,24},{24,32},{32,40},{40,48},{48,56},{56,64},{64,7... | collective-permute-start | bytes 98312 | tf_op jit(solution)/shard_map/ppermute | solution.py:33
  218.4 11.2 %collective-permute-start.30 = (f32[16,4,1,128]{3,0,2,1:T(8,128)S(1)}, f32[16,4,1,128]{3,0,2,1:T(8,128)S(1)}, u32[]{:S(2)}, u32[]{:S(2)}) collective-permute-start(f32[16,4,1,128]{3,0,2,1:T(8,128)S(1)} %get-tuple-element.102), channel_id=1, source_target_pairs={{8,0},{16,8},{24,16},{32,24},{40,32},{48,40},{56,48},{64,56},{72,6... | collective-permute-start | bytes 98312 | tf_op jit(solution)/shard_map/ppermute | solution.py:33
  221.9 7.7 collective-permute-start.31
  230.5 15.5 %collective-permute-start.33 = (f32[16,4,1,128]{3,0,2,1:T(8,128)S(1)}, f32[16,4,1,128]{3,0,2,1:T(8,128)S(1)}, u32[]{:S(2)}, u32[]{:S(2)}) collective-permute-start(f32[16,4,1,128]{3,0,2,1:T(8,128)S(1)} %get-tuple-element.97), channel_id=1, source_target_pairs={{0,8},{8,16},{16,24},{24,32},{32,40},{40,48},{48,56},{56,64},{64,7... | collective-permute-start | bytes 98312 | tf_op jit(solution)/shard_map/ppermute | solution.py:33
  234.7 11.2 %collective-permute-start.34 = (f32[16,4,1,128]{3,0,2,1:T(8,128)S(1)}, f32[16,4,1,128]{3,0,2,1:T(8,128)S(1)}, u32[]{:S(2)}, u32[]{:S(2)}) collective-permute-start(f32[16,4,1,128]{3,0,2,1:T(8,128)S(1)} %get-tuple-element.98), channel_id=1, source_target_pairs={{8,0},{16,8},{24,16},{32,24},{40,32},{48,40},{56,48},{64,56},{72,6... | collective-permute-start | bytes 98312 | tf_op jit(solution)/shard_map/ppermute | solution.py:33
  238.2 7.7 collective-permute-start.35
  343.1 14.3 %collective-permute-start.37 = (f32[16,4,1,128]{3,0,2,1:T(8,128)S(1)}, f32[16,4,1,128]{3,0,2,1:T(8,128)S(1)}, u32[]{:S(2)}, u32[]{:S(2)}) collective-permute-start(f32[16,4,1,128]{3,0,2,1:T(8,128)S(1)} %get-tuple-element.93), channel_id=1, source_target_pairs={{0,8},{8,16},{16,24},{24,32},{32,40},{40,48},{48,56},{56,64},{64,7... | collective-permute-start | bytes 98312 | tf_op jit(solution)/shard_map/ppermute | solution.py:33
  344.4 13.0 %collective-permute-start.38 = (f32[16,4,1,128]{3,0,2,1:T(8,128)S(1)}, f32[16,4,1,128]{3,0,2,1:T(8,128)S(1)}, u32[]{:S(2)}, u32[]{:S(2)}) collective-permute-start(f32[16,4,1,128]{3,0,2,1:T(8,128)S(1)} %get-tuple-element.94), channel_id=1, source_target_pairs={{8,0},{16,8},{24,16},{32,24},{40,32},{48,40},{56,48},{64,56},{72,6... | collective-permute-start | bytes 98312 | tf_op jit(solution)/shard_map/ppermute | solution.py:33
  345.8 7.1 collective-permute-start.36
  349.6 7.7 collective-permute-start.39
  358.2 15.5 %collective-permute-start.41 = (f32[16,4,1,128]{3,0,2,1:T(8,128)S(1)}, f32[16,4,1,128]{3,0,2,1:T(8,128)S(1)}, u32[]{:S(2)}, u32[]{:S(2)}) collective-permute-start(f32[16,4,1,128]{3,0,2,1:T(8,128)S(1)} %get-tuple-element.89), channel_id=1, source_target_pairs={{0,8},{8,16},{16,24},{24,32},{32,40},{40,48},{48,56},{56,64},{64,7... | collective-permute-start | bytes 98312 | tf_op jit(solution)/shard_map/ppermute | solution.py:33
  362.4 11.2 %collective-permute-start.42 = (f32[16,4,1,128]{3,0,2,1:T(8,128)S(1)}, f32[16,4,1,128]{3,0,2,1:T(8,128)S(1)}, u32[]{:S(2)}, u32[]{:S(2)}) collective-permute-start(f32[16,4,1,128]{3,0,2,1:T(8,128)S(1)} %get-tuple-element.90), channel_id=1, source_target_pairs={{8,0},{16,8},{24,16},{32,24},{40,32},{48,40},{56,48},{64,56},{72,6... | collective-permute-start | bytes 98312 | tf_op jit(solution)/shard_map/ppermute | solution.py:33
  365.9 7.7 collective-permute-start.43
  374.4 15.5 %collective-permute-start.45 = (f32[16,4,1,128]{3,0,2,1:T(8,128)S(1)}, f32[16,4,1,128]{3,0,2,1:T(8,128)S(1)}, u32[]{:S(2)}, u32[]{:S(2)}) collective-permute-start(f32[16,4,1,128]{3,0,2,1:T(8,128)S(1)} %get-tuple-element.85), channel_id=1, source_target_pairs={{0,8},{8,16},{16,24},{24,32},{32,40},{40,48},{48,56},{56,64},{64,7... | collective-permute-start | bytes 98312 | tf_op jit(solution)/shard_map/ppermute | solution.py:33
  378.7 11.2 %collective-permute-start.46 = (f32[16,4,1,128]{3,0,2,1:T(8,128)S(1)}, f32[16,4,1,128]{3,0,2,1:T(8,128)S(1)}, u32[]{:S(2)}, u32[]{:S(2)}) collective-permute-start(f32[16,4,1,128]{3,0,2,1:T(8,128)S(1)} %get-tuple-element.86), channel_id=1, source_target_pairs={{8,0},{16,8},{24,16},{32,24},{40,32},{48,40},{56,48},{64,56},{72,6... | collective-permute-start | bytes 98312 | tf_op jit(solution)/shard_map/ppermute | solution.py:33
  382.2 7.7 collective-permute-start.47
  390.9 15.5 %collective-permute-start.49 = (f32[16,4,1,128]{3,0,2,1:T(8,128)S(1)}, f32[16,4,1,128]{3,0,2,1:T(8,128)S(1)}, u32[]{:S(2)}, u32[]{:S(2)}) collective-permute-start(f32[16,4,1,128]{3,0,2,1:T(8,128)S(1)} %get-tuple-element.81), channel_id=1, source_target_pairs={{0,8},{8,16},{16,24},{24,32},{32,40},{40,48},{48,56},{56,64},{64,7... | collective-permute-start | bytes 98312 | tf_op jit(solution)/shard_map/ppermute | solution.py:33
  395.3 11.1 %collective-permute-start.50 = (f32[16,4,1,128]{3,0,2,1:T(8,128)S(1)}, f32[16,4,1,128]{3,0,2,1:T(8,128)S(1)}, u32[]{:S(2)}, u32[]{:S(2)}) collective-permute-start(f32[16,4,1,128]{3,0,2,1:T(8,128)S(1)} %get-tuple-element.82), channel_id=1, source_target_pairs={{8,0},{16,8},{24,16},{32,24},{40,32},{48,40},{56,48},{64,56},{72,6... | collective-permute-start | bytes 98312 | tf_op jit(solution)/shard_map/ppermute | solution.py:33
  398.7 7.7 collective-permute-start.51
  503.9 14.7 %collective-permute-start.53 = (f32[16,4,1,128]{3,0,2,1:T(8,128)S(1)}, f32[16,4,1,128]{3,0,2,1:T(8,128)S(1)}, u32[]{:S(2)}, u32[]{:S(2)}) collective-permute-start(f32[16,4,1,128]{3,0,2,1:T(8,128)S(1)} %get-tuple-element.77), channel_id=1, source_target_pairs={{0,8},{8,16},{16,24},{24,32},{32,40},{40,48},{48,56},{56,64},{64,7... | collective-permute-start | bytes 98312 | tf_op jit(solution)/shard_map/ppermute | solution.py:33
  505.2 13.4 %collective-permute-start.54 = (f32[16,4,1,128]{3,0,2,1:T(8,128)S(1)}, f32[16,4,1,128]{3,0,2,1:T(8,128)S(1)}, u32[]{:S(2)}, u32[]{:S(2)}) collective-permute-start(f32[16,4,1,128]{3,0,2,1:T(8,128)S(1)} %get-tuple-element.78), channel_id=1, source_target_pairs={{8,0},{16,8},{24,16},{32,24},{40,32},{48,40},{56,48},{64,56},{72,6... | collective-permute-start | bytes 98312 | tf_op jit(solution)/shard_map/ppermute | solution.py:33
  506.5 7.9 collective-permute-start.52
  510.8 7.7 collective-permute-start.55
  519.5 15.3 %collective-permute-start.57 = (f32[16,4,1,128]{3,0,2,1:T(8,128)S(1)}, f32[16,4,1,128]{3,0,2,1:T(8,128)S(1)}, u32[]{:S(2)}, u32[]{:S(2)}) collective-permute-start(f32[16,4,1,128]{3,0,2,1:T(8,128)S(1)} %get-tuple-element.73), channel_id=1, source_target_pairs={{0,8},{8,16},{16,24},{24,32},{32,40},{40,48},{48,56},{56,64},{64,7... | collective-permute-start | bytes 98312 | tf_op jit(solution)/shard_map/ppermute | solution.py:33
  523.8 11.1 %collective-permute-start.58 = (f32[16,4,1,128]{3,0,2,1:T(8,128)S(1)}, f32[16,4,1,128]{3,0,2,1:T(8,128)S(1)}, u32[]{:S(2)}, u32[]{:S(2)}) collective-permute-start(f32[16,4,1,128]{3,0,2,1:T(8,128)S(1)} %get-tuple-element.74), channel_id=1, source_target_pairs={{8,0},{16,8},{24,16},{32,24},{40,32},{48,40},{56,48},{64,56},{72,6... | collective-permute-start | bytes 98312 | tf_op jit(solution)/shard_map/ppermute | solution.py:33
  527.1 7.7 collective-permute-start.59
  535.8 15.3 %collective-permute-start.61 = (f32[16,4,1,128]{3,0,2,1:T(8,128)S(1)}, f32[16,4,1,128]{3,0,2,1:T(8,128)S(1)}, u32[]{:S(2)}, u32[]{:S(2)}) collective-permute-start(f32[16,4,1,128]{3,0,2,1:T(8,128)S(1)} %get-tuple-element.69), channel_id=1, source_target_pairs={{0,8},{8,16},{16,24},{24,32},{32,40},{40,48},{48,56},{56,64},{64,7... | collective-permute-start | bytes 98312 | tf_op jit(solution)/shard_map/ppermute | solution.py:33
  540.0 11.1 %collective-permute-start.62 = (f32[16,4,1,128]{3,0,2,1:T(8,128)S(1)}, f32[16,4,1,128]{3,0,2,1:T(8,128)S(1)}, u32[]{:S(2)}, u32[]{:S(2)}) collective-permute-start(f32[16,4,1,128]{3,0,2,1:T(8,128)S(1)} %get-tuple-element.70), channel_id=1, source_target_pairs={{8,0},{16,8},{24,16},{32,24},{40,32},{48,40},{56,48},{64,56},{72,6... | collective-permute-start | bytes 98312 | tf_op jit(solution)/shard_map/ppermute | solution.py:33
  543.4 7.7 collective-permute-start.63
  552.1 15.3 %collective-permute-start.65 = (f32[16,4,1,128]{3,0,2,1:T(8,128)S(1)}, f32[16,4,1,128]{3,0,2,1:T(8,128)S(1)}, u32[]{:S(2)}, u32[]{:S(2)}) collective-permute-start(f32[16,4,1,128]{3,0,2,1:T(8,128)S(1)} %get-tuple-element.65), channel_id=1, source_target_pairs={{0,8},{8,16},{16,24},{24,32},{32,40},{40,48},{48,56},{56,64},{64,7... | collective-permute-start | bytes 98312 | tf_op jit(solution)/shard_map/ppermute | solution.py:33
  556.3 11.1 %collective-permute-start.66 = (f32[16,4,1,128]{3,0,2,1:T(8,128)S(1)}, f32[16,4,1,128]{3,0,2,1:T(8,128)S(1)}, u32[]{:S(2)}, u32[]{:S(2)}) collective-permute-start(f32[16,4,1,128]{3,0,2,1:T(8,128)S(1)} %get-tuple-element.66), channel_id=1, source_target_pairs={{8,0},{16,8},{24,16},{32,24},{40,32},{48,40},{56,48},{64,56},{72,6... | collective-permute-start | bytes 98312 | tf_op jit(solution)/shard_map/ppermute | solution.py:33
  559.7 7.7 collective-permute-start.67
  660.0 14.4 %collective-permute-start.69 = (f32[16,4,1,128]{3,0,2,1:T(8,128)S(1)}, f32[16,4,1,128]{3,0,2,1:T(8,128)S(1)}, u32[]{:S(2)}, u32[]{:S(2)}) collective-permute-start(f32[16,4,1,128]{3,0,2,1:T(8,128)S(1)} %get-tuple-element.61), channel_id=1, source_target_pairs={{0,8},{8,16},{16,24},{24,32},{32,40},{40,48},{48,56},{56,64},{64,7... | collective-permute-start | bytes 98312 | tf_op jit(solution)/shard_map/ppermute | solution.py:33
  661.3 13.2 %collective-permute-start.70 = (f32[16,4,1,128]{3,0,2,1:T(8,128)S(1)}, f32[16,4,1,128]{3,0,2,1:T(8,128)S(1)}, u32[]{:S(2)}, u32[]{:S(2)}) collective-permute-start(f32[16,4,1,128]{3,0,2,1:T(8,128)S(1)} %get-tuple-element.62), channel_id=1, source_target_pairs={{8,0},{16,8},{24,16},{32,24},{40,32},{48,40},{56,48},{64,56},{72,6... | collective-permute-start | bytes 98312 | tf_op jit(solution)/shard_map/ppermute | solution.py:33
  662.6 7.4 collective-permute-start.68
  666.7 7.7 collective-permute-start.71
  675.4 15.3 %collective-permute-start.73 = (f32[16,4,1,128]{3,0,2,1:T(8,128)S(1)}, f32[16,4,1,128]{3,0,2,1:T(8,128)S(1)}, u32[]{:S(2)}, u32[]{:S(2)}) collective-permute-start(f32[16,4,1,128]{3,0,2,1:T(8,128)S(1)} %get-tuple-element.57), channel_id=1, source_target_pairs={{0,8},{8,16},{16,24},{24,32},{32,40},{40,48},{48,56},{56,64},{64,7... | collective-permute-start | bytes 98312 | tf_op jit(solution)/shard_map/ppermute | solution.py:33
  679.6 11.1 %collective-permute-start.74 = (f32[16,4,1,128]{3,0,2,1:T(8,128)S(1)}, f32[16,4,1,128]{3,0,2,1:T(8,128)S(1)}, u32[]{:S(2)}, u32[]{:S(2)}) collective-permute-start(f32[16,4,1,128]{3,0,2,1:T(8,128)S(1)} %get-tuple-element.58), channel_id=1, source_target_pairs={{8,0},{16,8},{24,16},{32,24},{40,32},{48,40},{56,48},{64,56},{72,6... | collective-permute-start | bytes 98312 | tf_op jit(solution)/shard_map/ppermute | solution.py:33
  683.0 7.7 collective-permute-start.75
  691.6 15.3 %collective-permute-start.77 = (f32[16,4,1,128]{3,0,2,1:T(8,128)S(1)}, f32[16,4,1,128]{3,0,2,1:T(8,128)S(1)}, u32[]{:S(2)}, u32[]{:S(2)}) collective-permute-start(f32[16,4,1,128]{3,0,2,1:T(8,128)S(1)} %get-tuple-element.53), channel_id=1, source_target_pairs={{0,8},{8,16},{16,24},{24,32},{32,40},{40,48},{48,56},{56,64},{64,7... | collective-permute-start | bytes 98312 | tf_op jit(solution)/shard_map/ppermute | solution.py:33
  695.9 11.1 %collective-permute-start.78 = (f32[16,4,1,128]{3,0,2,1:T(8,128)S(1)}, f32[16,4,1,128]{3,0,2,1:T(8,128)S(1)}, u32[]{:S(2)}, u32[]{:S(2)}) collective-permute-start(f32[16,4,1,128]{3,0,2,1:T(8,128)S(1)} %get-tuple-element.54), channel_id=1, source_target_pairs={{8,0},{16,8},{24,16},{32,24},{40,32},{48,40},{56,48},{64,56},{72,6... | collective-permute-start | bytes 98312 | tf_op jit(solution)/shard_map/ppermute | solution.py:33
  699.3 7.7 collective-permute-start.79
  707.9 15.3 %collective-permute-start.81 = (f32[16,4,1,128]{3,0,2,1:T(8,128)S(1)}, f32[16,4,1,128]{3,0,2,1:T(8,128)S(1)}, u32[]{:S(2)}, u32[]{:S(2)}) collective-permute-start(f32[16,4,1,128]{3,0,2,1:T(8,128)S(1)} %get-tuple-element.49), channel_id=1, source_target_pairs={{0,8},{8,16},{16,24},{24,32},{32,40},{40,48},{48,56},{56,64},{64,7... | collective-permute-start | bytes 98312 | tf_op jit(solution)/shard_map/ppermute | solution.py:33
  712.2 11.1 %collective-permute-start.82 = (f32[16,4,1,128]{3,0,2,1:T(8,128)S(1)}, f32[16,4,1,128]{3,0,2,1:T(8,128)S(1)}, u32[]{:S(2)}, u32[]{:S(2)}) collective-permute-start(f32[16,4,1,128]{3,0,2,1:T(8,128)S(1)} %get-tuple-element.50), channel_id=1, source_target_pairs={{8,0},{16,8},{24,16},{32,24},{40,32},{48,40},{56,48},{64,56},{72,6... | collective-permute-start | bytes 98312 | tf_op jit(solution)/shard_map/ppermute | solution.py:33
  715.5 7.7 collective-permute-start.83
  (22 other events, 135.4 us)
where the time goes:
time: 827 us; the launch traced here: 819 us
  blocking collectives  371 us (45%)
  starting transfers between devices  206 us (25%)
  waiting for transfers between devices  99.7 us (12%)
  other arithmetic  80.1 us (10%)
  local copies, waits for them, and re-layouts  29.8 us (4%)
  matrix products  28.9 us (3%)
    psum x5, blocking collectives, shards(): gram_all = lax.psum(local_gram, ('gx', 'gy'))  371 us
    ppermute x40, starting transfers between devices, halo_4(): lax.ppermute(last, axis, up)  123 us
    ppermute x40, waiting for transfers between devices, halo_4(): lax.ppermute(leading, axis, down)  81.7 us
    ppermute x40, starting transfers between devices, halo_4(): lax.ppermute(leading, axis, down)  71.1 us
    another operation x15, other arithmetic, small_solve(): lower = jnp.linalg.cholesky(normal)  32.6 us
    another operation x10, other arithmetic, small_solve(): y = jax.scipy.linalg.cho_solve((lower, True), right_side)  27.7 us
    unnamed x26, local copies, waits for them, and re-layouts  17.6 us
  transfers between devices with their start and end apart: 84, of which 34 were waited for; matrix products, arithmetic and copies ran while one was open for 2% of the time, Pallas kernels for 0%

commit v1 on v0

--- a/solution.py
+++ b/solution.py
@@ -90,7 +90,7 @@
             blocks.append(-apply_off(padded, terms) / diagonal)
         stacked = jnp.concatenate(blocks, 0).reshape(BASIS, -1)
         local_gram = jnp.dot(stacked, stacked.T, precision=hp)
-        gram_all = lax.psum(local_gram, ("gx", "gy"))
+        gram_all = lax.psum(lax.psum(local_gram, "gx"), "gy")
         y, coeffs = small_solve(gram_all)
         solution = solution + jnp.dot(y.T, stacked[: BASIS - RHS], precision=hp).reshape(shape)
         residual = jnp.dot(coeffs.T, stacked, precision=hp).reshape(shape)

time: 827 us -> 920 us (1.11)
  blocking collectives: 371 us -> 466 us
    psum x5 -> x10, blocking collectives: 371 us -> 466 us  [shards(): gram_all = lax.psum(lax.psum(local_gram, 'gx'), 'gy')]
  transfers between devices with their start and end apart: 84 -> 84, of which waited for: 34 -> 33; matrix products, arithmetic and copies ran while one was open for 2% -> 2% of each run, Pallas kernels for 0% -> 0%
where the time goes in v1:
time: 920 us; the launch traced here: 910 us
  blocking collectives  466 us (51%)
  starting transfers between devices  207 us (22%)
  waiting for transfers between devices  95 us (10%)
  other arithmetic  80.1 us (9%)
  local copies, waits for them, and re-layouts  29.7 us (3%)
  matrix products  28.9 us (3%)
    psum x10, blocking collectives, shards(): gram_all = lax.psum(lax.psum(local_gram, 'gx'), 'gy')  466 us
    ppermute x40, starting transfers between devices, halo_4(): lax.ppermute(last, axis, up)  119 us
    ppermute x40, waiting for transfers between devices, halo_4(): lax.ppermute(leading, axis, down)  79.5 us
    ppermute x40, starting transfers between devices, halo_4(): lax.ppermute(leading, axis, down)  75.8 us
    another operation x15, other arithmetic, small_solve(): lower = jnp.linalg.cholesky(normal)  32.6 us
    another operation x10, other arithmetic, small_solve(): y = jax.scipy.linalg.cho_solve((lower, True), right_side)  27.7 us
  transfers between devices with their start and end apart: 84, of which 33 were waited for; matrix products, arithmetic and copies ran while one was open for 2% of the time, Pallas kernels for 0%

profile of v1, /device:TPU:1, one launch (start us, length us, event | category | flops | bytes accessed | tf_op | source)
XLA Modules:
  0.0 909.8 jit_solution(18125513206362318506)
XLA Ops:
  1.4 4.0 collective-permute-start
  10.6 5.1 collective-permute-start.2
  17.6 3.3 collective-permute-done.3
  23.9 3.2 collective-permute-start.5
  34.1 4.4 collective-permute-done.7
  39.3 4.3 collective-permute-start.9
  50.4 4.4 collective-permute-done.11
  55.6 5.2 collective-permute-start.13
  67.6 4.4 collective-permute-done.15
  72.9 4.3 collective-permute-start.17
  83.9 4.4 collective-permute-done.19
  90.7 63.1 %psum.70 = f32[80,80]{1,0:T(8,128)S(1)} all-reduce(f32[80,80]{1,0:T(8,128)S(1)} %convolution_bitcast_fusion.4), channel_id=1, replica_groups=mesh['gx'=16,'gy'=8] {'gx'}, use_global_device_ids=true, to_apply=%region_0.1 | all-reduce | flops 6400 | bytes 51200 | tf_op jit(solution)/shard_map/psum | solution.py:93
  153.8 34.1 %psum.71 = f32[80,80]{1,0:T(8,128)S(1)} all-reduce(f32[80,80]{1,0:T(8,128)S(1)} %psum.70), channel_id=1, replica_groups=mesh['gx'=16,'gy'=8] {'gy'}, use_global_device_ids=true, to_apply=%region_1.2 | all-reduce | flops 6400 | bytes 51200 | tf_op jit(solution)/shard_map/psum | solution.py:93
  189.9 5.8 cholesky.89
  197.1 4.9 custom-call.11
  206.9 3.2 collective-permute-start.20
  210.1 3.2 collective-permute-start.23
  213.4 4.4 collective-permute-done.23
  218.6 4.3 collective-permute-start.25
  229.7 4.4 collective-permute-done.27
  234.9 4.3 collective-permute-start.29
  246.0 4.4 collective-permute-done.31
  251.2 4.3 collective-permute-start.33
  262.2 4.4 collective-permute-done.35
  270.1 58.6 %psum.72 = f32[80,80]{1,0:T(8,128)S(1)} all-reduce(f32[80,80]{1,0:T(8,128)S(1)} %convolution_bitcast_fusion.3), channel_id=1, replica_groups=mesh['gx'=16,'gy'=8] {'gx'}, use_global_device_ids=true, to_apply=%region_4.7 | all-reduce | flops 6400 | bytes 51200 | tf_op jit(solution)/shard_map/psum | solution.py:93
  328.6 33.6 %psum.73 = f32[80,80]{1,0:T(8,128)S(1)} all-reduce(f32[80,80]{1,0:T(8,128)S(1)} %psum.72), channel_id=1, replica_groups=mesh['gx'=16,'gy'=8] {'gy'}, use_global_device_ids=true, to_apply=%region_5.8 | all-reduce | flops 6400 | bytes 51200 | tf_op jit(solution)/shard_map/psum | solution.py:93
  366.5 5.8 cholesky.100
  373.7 4.9 custom-call.12
  384.8 3.2 collective-permute-start.36
  388.0 3.2 collective-permute-start.39
  391.3 4.4 collective-permute-done.39
  396.5 4.3 collective-permute-start.41
  407.6 4.4 collective-permute-done.43
  412.8 4.3 collective-permute-start.45
  423.9 4.4 collective-permute-done.47
  429.2 4.3 collective-permute-start.49
  448.0 58.3 %psum.74 = f32[80,80]{1,0:T(8,128)S(1)} all-reduce(f32[80,80]{1,0:T(8,128)S(1)} %convolution_bitcast_fusion.2), channel_id=1, replica_groups=mesh['gx'=16,'gy'=8] {'gx'}, use_global_device_ids=true, to_apply=%region_6.9 | all-reduce | flops 6400 | bytes 51200 | tf_op jit(solution)/shard_map/psum | solution.py:93
  506.3 33.5 %psum.75 = f32[80,80]{1,0:T(8,128)S(1)} all-reduce(f32[80,80]{1,0:T(8,128)S(1)} %psum.74), channel_id=1, replica_groups=mesh['gx'=16,'gy'=8] {'gy'}, use_global_device_ids=true, to_apply=%region_7.10 | all-reduce | flops 6400 | bytes 51200 | tf_op jit(solution)/shard_map/psum | solution.py:93
  544.2 5.8 cholesky.111
  551.4 4.9 custom-call.13
  562.6 3.2 collective-permute-start.52
  565.7 3.2 collective-permute-start.55
  570.2 3.3 collective-permute-done.55
  574.4 4.3 collective-permute-start.57
  586.3 3.8 collective-permute-done.59
  591.1 4.3 collective-permute-start.61
  602.2 4.2 collective-permute-done.63
  607.4 4.3 collective-permute-start.65
  625.1 58.6 %psum.76 = f32[80,80]{1,0:T(8,128)S(1)} all-reduce(f32[80,80]{1,0:T(8,128)S(1)} %convolution_bitcast_fusion.1), channel_id=1, replica_groups=mesh['gx'=16,'gy'=8] {'gx'}, use_global_device_ids=true, to_apply=%region_8.11 | all-reduce | flops 6400 | bytes 51200 | tf_op jit(solution)/shard_map/psum | solution.py:93
  683.7 33.5 %psum.77 = f32[80,80]{1,0:T(8,128)S(1)} all-reduce(f32[80,80]{1,0:T(8,128)S(1)} %psum.76), channel_id=1, replica_groups=mesh['gx'=16,'gy'=8] {'gy'}, use_global_device_ids=true, to_apply=%region_9.12 | all-reduce | flops 6400 | bytes 51200 | tf_op jit(solution)/shard_map/psum | solution.py:93
  719.2 5.8 cholesky.122
  726.4 4.9 custom-call.14
  739.4 3.2 collective-permute-start.71
  743.8 3.3 collective-permute-done.71
  748.1 4.3 collective-permute-start.73
  759.6 3.8 collective-permute-done.75
  764.3 4.3 collective-permute-start.77
  775.7 3.9 collective-permute-done.79
  780.6 4.3 collective-permute-start.81
  792.2 3.8 collective-permute-done.83
  798.4 58.6 %psum.78 = f32[80,80]{1,0:T(8,128)S(1)} all-reduce(f32[80,80]{1,0:T(8,128)S(1)} %convolution_bitcast_fusion), channel_id=1, replica_groups=mesh['gx'=16,'gy'=8] {'gx'}, use_global_device_ids=true, to_apply=%region_10.13 | all-reduce | flops 6400 | bytes 51200 | tf_op jit(solution)/shard_map/psum | solution.py:93
  856.9 33.6 %psum.79 = f32[80,80]{1,0:T(8,128)S(1)} all-reduce(f32[80,80]{1,0:T(8,128)S(1)} %psum.78), channel_id=1, replica_groups=mesh['gx'=16,'gy'=8] {'gy'}, use_global_device_ids=true, to_apply=%region_11.14 | all-reduce | flops 6400 | bytes 51200 | tf_op jit(solution)/shard_map/psum | solution.py:93
  892.5 5.8 cholesky.133
  899.7 4.9 custom-call.15
  (362 shorter events, 210.3 us)
Async XLA Ops:
  10.6 7.0 collective-permute-start.2
  23.9 14.6 %collective-permute-start.5 = (f32[16,4,1,128]{3,0,2,1:T(8,128)S(1)}, f32[16,4,1,128]{3,0,2,1:T(8,128)S(1)}, u32[]{:S(2)}, u32[]{:S(2)}) collective-permute-start(f32[16,4,1,128]{3,0,2,1:T(8,128)S(1)} %get-tuple-element.125), channel_id=1, source_target_pairs={{0,8},{8,16},{16,24},{24,32},{32,40},{40,48},{48,56},{56,64},{64,7... | collective-permute-start | bytes 98312 | tf_op jit(solution)/shard_map/ppermute | solution.py:33
  27.1 11.4 %collective-permute-start.6 = (f32[16,4,1,128]{3,0,2,1:T(8,128)S(1)}, f32[16,4,1,128]{3,0,2,1:T(8,128)S(1)}, u32[]{:S(2)}, u32[]{:S(2)}) collective-permute-start(f32[16,4,1,128]{3,0,2,1:T(8,128)S(1)} %get-tuple-element.126), channel_id=1, source_target_pairs={{8,0},{16,8},{24,16},{32,24},{40,32},{48,40},{56,48},{64,56},{72,6... | collective-permute-start | bytes 98312 | tf_op jit(solution)/shard_map/ppermute | solution.py:33
  30.8 7.7 collective-permute-start.7
  39.3 15.5 %collective-permute-start.9 = (f32[16,4,1,128]{3,0,2,1:T(8,128)S(1)}, f32[16,4,1,128]{3,0,2,1:T(8,128)S(1)}, u32[]{:S(2)}, u32[]{:S(2)}) collective-permute-start(f32[16,4,1,128]{3,0,2,1:T(8,128)S(1)} %get-tuple-element.121), channel_id=1, source_target_pairs={{0,8},{8,16},{16,24},{24,32},{32,40},{40,48},{48,56},{56,64},{64,7... | collective-permute-start | bytes 98312 | tf_op jit(solution)/shard_map/ppermute | solution.py:33
  43.6 11.2 %collective-permute-start.10 = (f32[16,4,1,128]{3,0,2,1:T(8,128)S(1)}, f32[16,4,1,128]{3,0,2,1:T(8,128)S(1)}, u32[]{:S(2)}, u32[]{:S(2)}) collective-permute-start(f32[16,4,1,128]{3,0,2,1:T(8,128)S(1)} %get-tuple-element.122), channel_id=1, source_target_pairs={{8,0},{16,8},{24,16},{32,24},{40,32},{48,40},{56,48},{64,56},{72,6... | collective-permute-start | bytes 98312 | tf_op jit(solution)/shard_map/ppermute | solution.py:33
  47.0 7.7 collective-permute-start.11
  55.6 16.4 %collective-permute-start.13 = (f32[16,4,1,128]{3,0,2,1:T(8,128)S(1)}, f32[16,4,1,128]{3,0,2,1:T(8,128)S(1)}, u32[]{:S(2)}, u32[]{:S(2)}) collective-permute-start(f32[16,4,1,128]{3,0,2,1:T(8,128)S(1)} %get-tuple-element.117), channel_id=1, source_target_pairs={{0,8},{8,16},{16,24},{24,32},{32,40},{40,48},{48,56},{56,64},{64,7... | collective-permute-start | bytes 98312 | tf_op jit(solution)/shard_map/ppermute | solution.py:33
  60.8 11.2 %collective-permute-start.14 = (f32[16,4,1,128]{3,0,2,1:T(8,128)S(1)}, f32[16,4,1,128]{3,0,2,1:T(8,128)S(1)}, u32[]{:S(2)}, u32[]{:S(2)}) collective-permute-start(f32[16,4,1,128]{3,0,2,1:T(8,128)S(1)} %get-tuple-element.118), channel_id=1, source_target_pairs={{8,0},{16,8},{24,16},{32,24},{40,32},{48,40},{56,48},{64,56},{72,6... | collective-permute-start | bytes 98312 | tf_op jit(solution)/shard_map/ppermute | solution.py:33
  64.3 7.7 collective-permute-start.15
  72.9 15.3 %collective-permute-start.17 = (f32[16,4,1,128]{3,0,2,1:T(8,128)S(1)}, f32[16,4,1,128]{3,0,2,1:T(8,128)S(1)}, u32[]{:S(2)}, u32[]{:S(2)}) collective-permute-start(f32[16,4,1,128]{3,0,2,1:T(8,128)S(1)} %get-tuple-element.113), channel_id=1, source_target_pairs={{0,8},{8,16},{16,24},{24,32},{32,40},{40,48},{48,56},{56,64},{64,7... | collective-permute-start | bytes 98312 | tf_op jit(solution)/shard_map/ppermute | solution.py:33
  77.2 11.1 %collective-permute-start.18 = (f32[16,4,1,128]{3,0,2,1:T(8,128)S(1)}, f32[16,4,1,128]{3,0,2,1:T(8,128)S(1)}, u32[]{:S(2)}, u32[]{:S(2)}) collective-permute-start(f32[16,4,1,128]{3,0,2,1:T(8,128)S(1)} %get-tuple-element.114), channel_id=1, source_target_pairs={{8,0},{16,8},{24,16},{32,24},{40,32},{48,40},{56,48},{64,56},{72,6... | collective-permute-start | bytes 98312 | tf_op jit(solution)/shard_map/ppermute | solution.py:33
  80.6 7.7 collective-permute-start.19
  204.2 13.6 %collective-permute-start.21 = (f32[16,4,1,128]{3,0,2,1:T(8,128)S(1)}, f32[16,4,1,128]{3,0,2,1:T(8,128)S(1)}, u32[]{:S(2)}, u32[]{:S(2)}) collective-permute-start(f32[16,4,1,128]{3,0,2,1:T(8,128)S(1)} %get-tuple-element.109), channel_id=1, source_target_pairs={{0,8},{8,16},{16,24},{24,32},{32,40},{40,48},{48,56},{56,64},{64,7... | collective-permute-start | bytes 98312 | tf_op jit(solution)/shard_map/ppermute | solution.py:33
  205.5 12.3 %collective-permute-start.22 = (f32[16,4,1,128]{3,0,2,1:T(8,128)S(1)}, f32[16,4,1,128]{3,0,2,1:T(8,128)S(1)}, u32[]{:S(2)}, u32[]{:S(2)}) collective-permute-start(f32[16,4,1,128]{3,0,2,1:T(8,128)S(1)} %get-tuple-element.110), channel_id=1, source_target_pairs={{8,0},{16,8},{24,16},{32,24},{40,32},{48,40},{56,48},{64,56},{72,6... | collective-permute-start | bytes 98312 | tf_op jit(solution)/shard_map/ppermute | solution.py:33
  210.1 7.7 collective-permute-start.23
  218.6 15.5 %collective-permute-start.25 = (f32[16,4,1,128]{3,0,2,1:T(8,128)S(1)}, f32[16,4,1,128]{3,0,2,1:T(8,128)S(1)}, u32[]{:S(2)}, u32[]{:S(2)}) collective-permute-start(f32[16,4,1,128]{3,0,2,1:T(8,128)S(1)} %get-tuple-element.105), channel_id=1, source_target_pairs={{0,8},{8,16},{16,24},{24,32},{32,40},{40,48},{48,56},{56,64},{64,7... | collective-permute-start | bytes 98312 | tf_op jit(solution)/shard_map/ppermute | solution.py:33
  222.9 11.2 %collective-permute-start.26 = (f32[16,4,1,128]{3,0,2,1:T(8,128)S(1)}, f32[16,4,1,128]{3,0,2,1:T(8,128)S(1)}, u32[]{:S(2)}, u32[]{:S(2)}) collective-permute-start(f32[16,4,1,128]{3,0,2,1:T(8,128)S(1)} %get-tuple-element.106), channel_id=1, source_target_pairs={{8,0},{16,8},{24,16},{32,24},{40,32},{48,40},{56,48},{64,56},{72,6... | collective-permute-start | bytes 98312 | tf_op jit(solution)/shard_map/ppermute | solution.py:33
  226.3 7.7 collective-permute-start.27
  234.9 15.5 %collective-permute-start.29 = (f32[16,4,1,128]{3,0,2,1:T(8,128)S(1)}, f32[16,4,1,128]{3,0,2,1:T(8,128)S(1)}, u32[]{:S(2)}, u32[]{:S(2)}) collective-permute-start(f32[16,4,1,128]{3,0,2,1:T(8,128)S(1)} %get-tuple-element.101), channel_id=1, source_target_pairs={{0,8},{8,16},{16,24},{24,32},{32,40},{40,48},{48,56},{56,64},{64,7... | collective-permute-start | bytes 98312 | tf_op jit(solution)/shard_map/ppermute | solution.py:33
  239.2 11.2 %collective-permute-start.30 = (f32[16,4,1,128]{3,0,2,1:T(8,128)S(1)}, f32[16,4,1,128]{3,0,2,1:T(8,128)S(1)}, u32[]{:S(2)}, u32[]{:S(2)}) collective-permute-start(f32[16,4,1,128]{3,0,2,1:T(8,128)S(1)} %get-tuple-element.102), channel_id=1, source_target_pairs={{8,0},{16,8},{24,16},{32,24},{40,32},{48,40},{56,48},{64,56},{72,6... | collective-permute-start | bytes 98312 | tf_op jit(solution)/shard_map/ppermute | solution.py:33
  242.6 7.7 collective-permute-start.31
  251.2 15.5 %collective-permute-start.33 = (f32[16,4,1,128]{3,0,2,1:T(8,128)S(1)}, f32[16,4,1,128]{3,0,2,1:T(8,128)S(1)}, u32[]{:S(2)}, u32[]{:S(2)}) collective-permute-start(f32[16,4,1,128]{3,0,2,1:T(8,128)S(1)} %get-tuple-element.97), channel_id=1, source_target_pairs={{0,8},{8,16},{16,24},{24,32},{32,40},{40,48},{48,56},{56,64},{64,7... | collective-permute-start | bytes 98312 | tf_op jit(solution)/shard_map/ppermute | solution.py:33
  255.4 11.2 %collective-permute-start.34 = (f32[16,4,1,128]{3,0,2,1:T(8,128)S(1)}, f32[16,4,1,128]{3,0,2,1:T(8,128)S(1)}, u32[]{:S(2)}, u32[]{:S(2)}) collective-permute-start(f32[16,4,1,128]{3,0,2,1:T(8,128)S(1)} %get-tuple-element.98), channel_id=1, source_target_pairs={{8,0},{16,8},{24,16},{32,24},{40,32},{48,40},{56,48},{64,56},{72,6... | collective-permute-start | bytes 98312 | tf_op jit(solution)/shard_map/ppermute | solution.py:33
  258.9 7.7 collective-permute-start.35
  382.1 13.6 %collective-permute-start.37 = (f32[16,4,1,128]{3,0,2,1:T(8,128)S(1)}, f32[16,4,1,128]{3,0,2,1:T(8,128)S(1)}, u32[]{:S(2)}, u32[]{:S(2)}) collective-permute-start(f32[16,4,1,128]{3,0,2,1:T(8,128)S(1)} %get-tuple-element.93), channel_id=1, source_target_pairs={{0,8},{8,16},{16,24},{24,32},{32,40},{40,48},{48,56},{56,64},{64,7... | collective-permute-start | bytes 98312 | tf_op jit(solution)/shard_map/ppermute | solution.py:33
  383.4 12.3 %collective-permute-start.38 = (f32[16,4,1,128]{3,0,2,1:T(8,128)S(1)}, f32[16,4,1,128]{3,0,2,1:T(8,128)S(1)}, u32[]{:S(2)}, u32[]{:S(2)}) collective-permute-start(f32[16,4,1,128]{3,0,2,1:T(8,128)S(1)} %get-tuple-element.94), channel_id=1, source_target_pairs={{8,0},{16,8},{24,16},{32,24},{40,32},{48,40},{56,48},{64,56},{72,6... | collective-permute-start | bytes 98312 | tf_op jit(solution)/shard_map/ppermute | solution.py:33
  388.0 7.7 collective-permute-start.39
  396.5 15.5 %collective-permute-start.41 = (f32[16,4,1,128]{3,0,2,1:T(8,128)S(1)}, f32[16,4,1,128]{3,0,2,1:T(8,128)S(1)}, u32[]{:S(2)}, u32[]{:S(2)}) collective-permute-start(f32[16,4,1,128]{3,0,2,1:T(8,128)S(1)} %get-tuple-element.89), channel_id=1, source_target_pairs={{0,8},{8,16},{16,24},{24,32},{32,40},{40,48},{48,56},{56,64},{64,7... | collective-permute-start | bytes 98312 | tf_op jit(solution)/shard_map/ppermute | solution.py:33
  400.8 11.2 %collective-permute-start.42 = (f32[16,4,1,128]{3,0,2,1:T(8,128)S(1)}, f32[16,4,1,128]{3,0,2,1:T(8,128)S(1)}, u32[]{:S(2)}, u32[]{:S(2)}) collective-permute-start(f32[16,4,1,128]{3,0,2,1:T(8,128)S(1)} %get-tuple-element.90), channel_id=1, source_target_pairs={{8,0},{16,8},{24,16},{32,24},{40,32},{48,40},{56,48},{64,56},{72,6... | collective-permute-start | bytes 98312 | tf_op jit(solution)/shard_map/ppermute | solution.py:33
  404.2 7.7 collective-permute-start.43
  412.8 15.5 %collective-permute-start.45 = (f32[16,4,1,128]{3,0,2,1:T(8,128)S(1)}, f32[16,4,1,128]{3,0,2,1:T(8,128)S(1)}, u32[]{:S(2)}, u32[]{:S(2)}) collective-permute-start(f32[16,4,1,128]{3,0,2,1:T(8,128)S(1)} %get-tuple-element.85), channel_id=1, source_target_pairs={{0,8},{8,16},{16,24},{24,32},{32,40},{40,48},{48,56},{56,64},{64,7... | collective-permute-start | bytes 98312 | tf_op jit(solution)/shard_map/ppermute | solution.py:33
  417.1 11.2 %collective-permute-start.46 = (f32[16,4,1,128]{3,0,2,1:T(8,128)S(1)}, f32[16,4,1,128]{3,0,2,1:T(8,128)S(1)}, u32[]{:S(2)}, u32[]{:S(2)}) collective-permute-start(f32[16,4,1,128]{3,0,2,1:T(8,128)S(1)} %get-tuple-element.86), channel_id=1, source_target_pairs={{8,0},{16,8},{24,16},{32,24},{40,32},{48,40},{56,48},{64,56},{72,6... | collective-permute-start | bytes 98312 | tf_op jit(solution)/shard_map/ppermute | solution.py:33
  420.5 7.7 collective-permute-start.47
  429.2 15.3 %collective-permute-start.49 = (f32[16,4,1,128]{3,0,2,1:T(8,128)S(1)}, f32[16,4,1,128]{3,0,2,1:T(8,128)S(1)}, u32[]{:S(2)}, u32[]{:S(2)}) collective-permute-start(f32[16,4,1,128]{3,0,2,1:T(8,128)S(1)} %get-tuple-element.81), channel_id=1, source_target_pairs={{0,8},{8,16},{16,24},{24,32},{32,40},{40,48},{48,56},{56,64},{64,7... | collective-permute-start | bytes 98312 | tf_op jit(solution)/shard_map/ppermute | solution.py:33
  433.5 11.1 %collective-permute-start.50 = (f32[16,4,1,128]{3,0,2,1:T(8,128)S(1)}, f32[16,4,1,128]{3,0,2,1:T(8,128)S(1)}, u32[]{:S(2)}, u32[]{:S(2)}) collective-permute-start(f32[16,4,1,128]{3,0,2,1:T(8,128)S(1)} %get-tuple-element.82), channel_id=1, source_target_pairs={{8,0},{16,8},{24,16},{32,24},{40,32},{48,40},{56,48},{64,56},{72,6... | collective-permute-start | bytes 98312 | tf_op jit(solution)/shard_map/ppermute | solution.py:33
  434.8 7.1 collective-permute-start.48
  436.8 7.7 collective-permute-start.51
  560.0 13.5 %collective-permute-start.53 = (f32[16,4,1,128]{3,0,2,1:T(8,128)S(1)}, f32[16,4,1,128]{3,0,2,1:T(8,128)S(1)}, u32[]{:S(2)}, u32[]{:S(2)}) collective-permute-start(f32[16,4,1,128]{3,0,2,1:T(8,128)S(1)} %get-tuple-element.77), channel_id=1, source_target_pairs={{0,8},{8,16},{16,24},{24,32},{32,40},{40,48},{48,56},{56,64},{64,7... | collective-permute-start | bytes 98312 | tf_op jit(solution)/shard_map/ppermute | solution.py:33
  561.3 12.2 %collective-permute-start.54 = (f32[16,4,1,128]{3,0,2,1:T(8,128)S(1)}, f32[16,4,1,128]{3,0,2,1:T(8,128)S(1)}, u32[]{:S(2)}, u32[]{:S(2)}) collective-permute-start(f32[16,4,1,128]{3,0,2,1:T(8,128)S(1)} %get-tuple-element.78), channel_id=1, source_target_pairs={{8,0},{16,8},{24,16},{32,24},{40,32},{48,40},{56,48},{64,56},{72,6... | collective-permute-start | bytes 98312 | tf_op jit(solution)/shard_map/ppermute | solution.py:33
  562.6 7.5 collective-permute-start.52
  565.7 7.7 collective-permute-start.55
  574.4 15.7 %collective-permute-start.57 = (f32[16,4,1,128]{3,0,2,1:T(8,128)S(1)}, f32[16,4,1,128]{3,0,2,1:T(8,128)S(1)}, u32[]{:S(2)}, u32[]{:S(2)}) collective-permute-start(f32[16,4,1,128]{3,0,2,1:T(8,128)S(1)} %get-tuple-element.73), channel_id=1, source_target_pairs={{0,8},{8,16},{16,24},{24,32},{32,40},{40,48},{48,56},{56,64},{64,7... | collective-permute-start | bytes 98312 | tf_op jit(solution)/shard_map/ppermute | solution.py:33
  578.7 11.5 %collective-permute-start.58 = (f32[16,4,1,128]{3,0,2,1:T(8,128)S(1)}, f32[16,4,1,128]{3,0,2,1:T(8,128)S(1)}, u32[]{:S(2)}, u32[]{:S(2)}) collective-permute-start(f32[16,4,1,128]{3,0,2,1:T(8,128)S(1)} %get-tuple-element.74), channel_id=1, source_target_pairs={{8,0},{16,8},{24,16},{32,24},{40,32},{48,40},{56,48},{64,56},{72,6... | collective-permute-start | bytes 98312 | tf_op jit(solution)/shard_map/ppermute | solution.py:33
  582.4 7.7 collective-permute-start.59
  591.1 15.3 %collective-permute-start.61 = (f32[16,4,1,128]{3,0,2,1:T(8,128)S(1)}, f32[16,4,1,128]{3,0,2,1:T(8,128)S(1)}, u32[]{:S(2)}, u32[]{:S(2)}) collective-permute-start(f32[16,4,1,128]{3,0,2,1:T(8,128)S(1)} %get-tuple-element.69), channel_id=1, source_target_pairs={{0,8},{8,16},{16,24},{24,32},{32,40},{40,48},{48,56},{56,64},{64,7... | collective-permute-start | bytes 98312 | tf_op jit(solution)/shard_map/ppermute | solution.py:33
  595.4 11.1 %collective-permute-start.62 = (f32[16,4,1,128]{3,0,2,1:T(8,128)S(1)}, f32[16,4,1,128]{3,0,2,1:T(8,128)S(1)}, u32[]{:S(2)}, u32[]{:S(2)}) collective-permute-start(f32[16,4,1,128]{3,0,2,1:T(8,128)S(1)} %get-tuple-element.70), channel_id=1, source_target_pairs={{8,0},{16,8},{24,16},{32,24},{40,32},{48,40},{56,48},{64,56},{72,6... | collective-permute-start | bytes 98312 | tf_op jit(solution)/shard_map/ppermute | solution.py:33
  598.7 7.7 collective-permute-start.63
  607.4 15.3 %collective-permute-start.65 = (f32[16,4,1,128]{3,0,2,1:T(8,128)S(1)}, f32[16,4,1,128]{3,0,2,1:T(8,128)S(1)}, u32[]{:S(2)}, u32[]{:S(2)}) collective-permute-start(f32[16,4,1,128]{3,0,2,1:T(8,128)S(1)} %get-tuple-element.65), channel_id=1, source_target_pairs={{0,8},{8,16},{16,24},{24,32},{32,40},{40,48},{48,56},{56,64},{64,7... | collective-permute-start | bytes 98312 | tf_op jit(solution)/shard_map/ppermute | solution.py:33
  611.7 11.1 %collective-permute-start.66 = (f32[16,4,1,128]{3,0,2,1:T(8,128)S(1)}, f32[16,4,1,128]{3,0,2,1:T(8,128)S(1)}, u32[]{:S(2)}, u32[]{:S(2)}) collective-permute-start(f32[16,4,1,128]{3,0,2,1:T(8,128)S(1)} %get-tuple-element.66), channel_id=1, source_target_pairs={{8,0},{16,8},{24,16},{32,24},{40,32},{48,40},{56,48},{64,56},{72,6... | collective-permute-start | bytes 98312 | tf_op jit(solution)/shard_map/ppermute | solution.py:33
  615.0 7.7 collective-permute-start.67
  733.6 13.5 %collective-permute-start.69 = (f32[16,4,1,128]{3,0,2,1:T(8,128)S(1)}, f32[16,4,1,128]{3,0,2,1:T(8,128)S(1)}, u32[]{:S(2)}, u32[]{:S(2)}) collective-permute-start(f32[16,4,1,128]{3,0,2,1:T(8,128)S(1)} %get-tuple-element.61), channel_id=1, source_target_pairs={{0,8},{8,16},{16,24},{24,32},{32,40},{40,48},{48,56},{56,64},{64,7... | collective-permute-start | bytes 98312 | tf_op jit(solution)/shard_map/ppermute | solution.py:33
  734.9 12.2 %collective-permute-start.70 = (f32[16,4,1,128]{3,0,2,1:T(8,128)S(1)}, f32[16,4,1,128]{3,0,2,1:T(8,128)S(1)}, u32[]{:S(2)}, u32[]{:S(2)}) collective-permute-start(f32[16,4,1,128]{3,0,2,1:T(8,128)S(1)} %get-tuple-element.62), channel_id=1, source_target_pairs={{8,0},{16,8},{24,16},{32,24},{40,32},{48,40},{56,48},{64,56},{72,6... | collective-permute-start | bytes 98312 | tf_op jit(solution)/shard_map/ppermute | solution.py:33
  736.2 7.5 collective-permute-start.68
  739.4 7.7 collective-permute-start.71
  748.1 15.3 %collective-permute-start.73 = (f32[16,4,1,128]{3,0,2,1:T(8,128)S(1)}, f32[16,4,1,128]{3,0,2,1:T(8,128)S(1)}, u32[]{:S(2)}, u32[]{:S(2)}) collective-permute-start(f32[16,4,1,128]{3,0,2,1:T(8,128)S(1)} %get-tuple-element.57), channel_id=1, source_target_pairs={{0,8},{8,16},{16,24},{24,32},{32,40},{40,48},{48,56},{56,64},{64,7... | collective-permute-start | bytes 98312 | tf_op jit(solution)/shard_map/ppermute | solution.py:33
  752.3 11.1 %collective-permute-start.74 = (f32[16,4,1,128]{3,0,2,1:T(8,128)S(1)}, f32[16,4,1,128]{3,0,2,1:T(8,128)S(1)}, u32[]{:S(2)}, u32[]{:S(2)}) collective-permute-start(f32[16,4,1,128]{3,0,2,1:T(8,128)S(1)} %get-tuple-element.58), channel_id=1, source_target_pairs={{8,0},{16,8},{24,16},{32,24},{40,32},{48,40},{56,48},{64,56},{72,6... | collective-permute-start | bytes 98312 | tf_op jit(solution)/shard_map/ppermute | solution.py:33
  755.7 7.7 collective-permute-start.75
  764.3 15.3 %collective-permute-start.77 = (f32[16,4,1,128]{3,0,2,1:T(8,128)S(1)}, f32[16,4,1,128]{3,0,2,1:T(8,128)S(1)}, u32[]{:S(2)}, u32[]{:S(2)}) collective-permute-start(f32[16,4,1,128]{3,0,2,1:T(8,128)S(1)} %get-tuple-element.53), channel_id=1, source_target_pairs={{0,8},{8,16},{16,24},{24,32},{32,40},{40,48},{48,56},{56,64},{64,7... | collective-permute-start | bytes 98312 | tf_op jit(solution)/shard_map/ppermute | solution.py:33
  768.6 11.1 %collective-permute-start.78 = (f32[16,4,1,128]{3,0,2,1:T(8,128)S(1)}, f32[16,4,1,128]{3,0,2,1:T(8,128)S(1)}, u32[]{:S(2)}, u32[]{:S(2)}) collective-permute-start(f32[16,4,1,128]{3,0,2,1:T(8,128)S(1)} %get-tuple-element.54), channel_id=1, source_target_pairs={{8,0},{16,8},{24,16},{32,24},{40,32},{48,40},{56,48},{64,56},{72,6... | collective-permute-start | bytes 98312 | tf_op jit(solution)/shard_map/ppermute | solution.py:33
  772.0 7.7 collective-permute-start.79
  780.6 15.3 %collective-permute-start.81 = (f32[16,4,1,128]{3,0,2,1:T(8,128)S(1)}, f32[16,4,1,128]{3,0,2,1:T(8,128)S(1)}, u32[]{:S(2)}, u32[]{:S(2)}) collective-permute-start(f32[16,4,1,128]{3,0,2,1:T(8,128)S(1)} %get-tuple-element.49), channel_id=1, source_target_pairs={{0,8},{8,16},{16,24},{24,32},{32,40},{40,48},{48,56},{56,64},{64,7... | collective-permute-start | bytes 98312 | tf_op jit(solution)/shard_map/ppermute | solution.py:33
  784.9 11.1 %collective-permute-start.82 = (f32[16,4,1,128]{3,0,2,1:T(8,128)S(1)}, f32[16,4,1,128]{3,0,2,1:T(8,128)S(1)}, u32[]{:S(2)}, u32[]{:S(2)}) collective-permute-start(f32[16,4,1,128]{3,0,2,1:T(8,128)S(1)} %get-tuple-element.50), channel_id=1, source_target_pairs={{8,0},{16,8},{24,16},{32,24},{40,32},{48,40},{56,48},{64,56},{72,6... | collective-permute-start | bytes 98312 | tf_op jit(solution)/shard_map/ppermute | solution.py:33
  788.2 7.7 collective-permute-start.83
  (22 other events, 134.8 us)
